TPU v7x, 256 devices: a whole 4x4x8 slice. The times are simulated.
256 devices in a mesh: lon: 32 (over y, z), lat: 8 (over x, core).
Axes of the slice: x: 4, y: 4, z: 8, core: 2. Of those that a mesh axis runs over, the one named last changes fastest.
Arguments:
- fields: float32 [129, 6, 128, 1024], P(None, None, 'lat', 'lon'), may hold values from -38 to 38
Outputs:
- koopman_modes: float32 [30, 128, 1024, 128], P(None, 'lat', 'lon')
- forward_operator: float32 [128, 128], replicated
- backward_operator: float32 [128, 128], replicated
All inputs are finite; a program needn't handle non-finite values.
Results may differ from a plain program's by a relative error of at most 0.0001.
Values sent between devices are 32-bit elements; how exact they have to be, the bound alone decides.
A program may use at most 64 MiB of HBM per device.

v0:
```python
import jax
import jax.numpy as jnp
from jax import lax
from jax.sharding import PartitionSpec as P


def with_halo(block, sides, width, periodic):
    for axis, dim in sides:
        count = lax.axis_size(axis)
        forward = [(i, i + 1) for i in range(count - 1)]
        if periodic:
            forward.append((count - 1, 0))
        backward = [(target, source) for source, target in forward]
        low = lax.ppermute(
            lax.slice_in_dim(block, block.shape[dim] - width, None, axis=dim), axis, forward
        )
        high = lax.ppermute(lax.slice_in_dim(block, 0, width, axis=dim), axis, backward)
        block = jnp.concatenate([low, block, high], axis=dim)
    return block


def reduced_operators(upper_factor, gram_total):
    snap_count = upper_factor.shape[0] - 1
    head_block = upper_factor[:snap_count, :snap_count]
    forward_operator = jax.scipy.linalg.solve_triangular(
        head_block.T, upper_factor[:snap_count, 1:].T, lower=True
    ).T
    back_factor = jnp.linalg.cholesky(gram_total[1:, 1:])
    mixed_block = jax.scipy.linalg.solve_triangular(
        back_factor, gram_total[1:, :snap_count], lower=True
    )
    backward_operator = jax.scipy.linalg.solve_triangular(back_factor, mixed_block.T, lower=True).T
    return (forward_operator, backward_operator)


def shards(fields):
    states = fields.shape[0]
    snap_count = states - 1
    channels = fields.shape[1]
    band_rows = fields.shape[2]
    sector_cols = fields.shape[3]
    lon_padded = with_halo(fields, (("lon", 3),), 1, True)
    lat_padded = with_halo(fields, (("lat", 2),), 1, False)
    neighbour_list = (
        lat_padded[:, :, :-2],
        lat_padded[:, :, 2:],
        lon_padded[:, :, :, :-2],
        lon_padded[:, :, :, 2:],
    )
    slab_list = [fields] + [fields * neighbour for neighbour in neighbour_list]
    rows_total = (
        5 * channels * band_rows * lax.axis_size("lat") * sector_cols * lax.axis_size("lon")
    )
    gram_local = jnp.zeros((states, states), jnp.float32)
    for feature_slab in slab_list:
        flat_rows = feature_slab.reshape(states, -1)
        gram_local = gram_local + jnp.dot(flat_rows, flat_rows.T, precision=lax.Precision.HIGHEST)
    gram_local = gram_local / rows_total
    gram_total = lax.psum(gram_local, ("lon", "lat"))
    upper_factor = jnp.linalg.cholesky(gram_total).T
    forward_operator, backward_operator = reduced_operators(upper_factor, gram_total)
    head_block = upper_factor[:snap_count, :snap_count]
    mode_parts = []
    for feature_slab in slab_list:
        flat_rows = feature_slab.reshape(states, -1)[:snap_count]
        solved = jax.scipy.linalg.solve_triangular(head_block.T, flat_rows, lower=True)
        mode_parts.append(
            solved.reshape(snap_count, channels, band_rows, sector_cols).transpose(1, 2, 3, 0)
        )
    koopman_modes = jnp.concatenate(mode_parts, axis=0)
    return (koopman_modes, forward_operator, backward_operator)


def solution(mesh):
    placed = (P(None, None, "lat", "lon"),)
    return jax.shard_map(
        shards,
        mesh=mesh,
        in_specs=placed,
        out_specs=(P(None, "lat", "lon", None), P(), P()),
        check_vma=False,
    )
```

profile of v0, /device:TPU:1, one launch (start us, length us, event | category | flops | bytes accessed | tf_op | source)
XLA Modules:
  0.0 388.6 jit_solution(6079797568631075508)
XLA Ops:
  7.2 1.5 fusion.35
  8.8 8.9 %collective-permute-start.3 = (f32[129,6,16,1]{0,2,3,1:T(8,128)S(1)}, f32[129,6,16,1]{0,2,3,1:T(8,128)S(1)}, u32[]{:S(2)}, u32[]{:S(2)}) collective-permute-start(f32[129,6,16,1]{0,2,3,1:T(8,128)S(1)} %copy.74), channel_id=1, source_target_pairs={{8,0},{16,8},{24,16},{32,24},{40,32},{48,40},{56,48},{64,56},{72,6... | collective-permute-start | bytes 148616 | tf_op jit(solution)/shard_map/ppermute | solution.py:17
  17.8 1.1 fusion.34
  18.8 4.0 %collective-permute-start = (f32[129,6,1,32]{0,3,2,1:T(8,128)S(1)}, f32[129,6,1,32]{0,3,2,1:T(8,128)S(1)}, u32[]{:S(2)}, u32[]{:S(2)}) collective-permute-start(f32[129,6,1,32]{0,3,2,1:T(8,128)S(1)} %get-tuple-element.18), channel_id=1, source_target_pairs={{0,1},{1,2},{2,3},{3,4},{4,5},{5,6},{6,7},{8,9},{9,10},{10,11},{11... | collective-permute-start | bytes 297224 | tf_op jit(solution)/shard_map/ppermute | solution.py:14
  22.8 2.2 collective-permute-start.1
  25.0 8.0 %convolution_bitcast_fusion.4 = f32[129,129]{0,1:T(8,128)S(1)} fusion(f32[129,6,16,32]{0,3,2,1:T(8,128)} %param.5), kind=kOutput, calls=%fused_computation.12 | convolution fusion | flops 613453824 | bytes 1651716 | tf_op jit(solution)/shard_map/dot_general | solution.py:57
  33.3 2.5 fusion.3
  35.8 5.1 %convolution_bitcast_fusion.2 = f32[129,129]{0,1:T(8,128)S(1)} fusion(f32[129,6,16,32]{0,3,2,1:T(8,128)S(1)} %get-tuple-element.15), kind=kOutput, calls=%fused_computation.10 | convolution fusion | flops 613453824 | bytes 1651716 | tf_op jit(solution)/shard_map/dot_general | solution.py:57
  41.0 5.1 %convolution_bitcast_fusion.1 = f32[129,129]{0,1:T(8,128)S(1)} fusion(f32[129,6,16,32]{0,3,2,1:T(8,128)S(1)} %get-tuple-element.16), kind=kOutput, calls=%fused_computation.9 | convolution fusion | flops 613453824 | bytes 1651716 | tf_op jit(solution)/shard_map/dot_general | solution.py:57
  46.1 5.3 %convolution_bitcast_fusion = f32[129,129]{0,1:T(8,128)S(1)} fusion(f32[129,6,16,32]{0,3,2,1:T(8,128)S(1)} %get-tuple-element.17), kind=kOutput, calls=%fused_computation.8 | convolution fusion | flops 613453824 | bytes 1651716 | tf_op jit(solution)/shard_map/dot_general | solution.py:57
  51.5 5.8 %fusion.8 = f32[129,129]{0,1:T(8,128)} fusion(f32[129,129]{0,1:T(8,128)S(1)} %convolution_bitcast_fusion, f32[129,129]{0,1:T(8,128)S(1)} %convolution_bitcast_fusion.1, f32[129,129]{0,1:T(8,128)S(1)} %convolution_bitcast_fusion.2, f32[129,129]{0,1:T(8,128)S(1)} %convolution_bitcast_fusion.4, f32[129,6,16,32]{0,3,2,1:T(8,128)S(1)} %get-tuple-element.14), kind=kOutput, calls=%fused_computation.17 | convolution fusion | flops 613537024 | bytes 1917972 | tf_op jit(solution)/shard_map/dot_general | solution.py:57
  57.4 1.7 slice.141
  59.9 0.8 copy-done.2
  60.7 1.3 slice.143
  62.0 1.3 slice.140
  63.3 239.0 %all-reduce.3.cloned.1.call-done = f32[129,129]{0,1:T(8,128)} async-done(((f32[129,129]{0,1:T(8,128)}), f32[129,129]{0,1:T(8,128)}) %all-reduce.3.cloned.1.call-update) | async-done | bytes 66580 | tf_op jit(solution)/shard_map/psum | solution.py:59
  302.3 1.0 copy.45
  303.3 0.9 fusion.9
  304.8 1.0 slice.145
  305.9 1.0 fusion.16
  306.9 11.7 %cholesky.144 = f32[128,128]{1,0:T(8,128)S(1)} custom-call(f32[128,128]{1,0:T(8,128)S(1)} %fusion.16), custom_call_target="Cholesky" | custom-call | tf_op jit(solution)/shard_map/jit(cholesky)/cholesky | solution.py:28
  320.0 10.2 %custom-call.31 = f32[1,128,128]{1,2,0:T(8,128)S(1)} custom-call(f32[1,128,128]{2,1,0:T(8,128)S(1)} %fusion.10), custom_call_target="InvertDiagBlocksLowerTriangular" | custom-call | tf_op jit(solution)/shard_map/jit(_solve_triangular)/triangular_solve | solution.py:32
  330.1 1.2 convolution_bitcast_fusion.6
  332.5 11.7 %cholesky.63 = f32[128,128]{1,0:T(8,128)S(1)} custom-call(f32[128,128]{1,0:T(8,128)S(1)} %copy.46), custom_call_target="Cholesky" | custom-call | tf_op jit(solution)/shard_map/jit(cholesky)/cholesky | solution.py:60
  345.0 9.8 %custom-call.17 = f32[1,128,128]{1,2,0:T(8,128)S(1)} custom-call(f32[1,128,128]{2,1,0:T(8,128)S(1)} %get-tuple-element.23), custom_call_target="InvertDiagBlocksLowerTriangular" | custom-call | tf_op jit(solution)/shard_map/jit(cholesky)/cholesky | solution.py:60
  358.0 9.8 %custom-call.24 = f32[1,128,128]{1,2,0:T(8,128)S(1)} custom-call(f32[1,128,128]{2,1,0:T(8,128)S(1)} %fusion.13), custom_call_target="InvertDiagBlocksLowerTriangular" | custom-call | tf_op jit(solution)/shard_map/jit(_solve_triangular)/triangular_solve | solution.py:66
  368.9 2.8 fusion.24
  371.7 1.4 fusion.22
  373.1 1.4 fusion.20
  374.5 1.4 fusion.18
  375.9 1.4 fusion.26
  378.3 3.2 copy-done.9
  (57 shorter events, 8.4 us)
Async XLA Ops:
  7.2 295.1 %all-reduce.3.cloned.1.call-start = ((), (), s32[]{:S(2)}) async-start(), calls=%async_computation | async-start | bytes 278528 | tf_op jit(solution)/shard_map/psum | solution.py:59
  8.8 24.3 %collective-permute-start.3 = (f32[129,6,16,1]{0,2,3,1:T(8,128)S(1)}, f32[129,6,16,1]{0,2,3,1:T(8,128)S(1)}, u32[]{:S(2)}, u32[]{:S(2)}) collective-permute-start(f32[129,6,16,1]{0,2,3,1:T(8,128)S(1)} %copy.74), channel_id=1, source_target_pairs={{8,0},{16,8},{24,16},{32,24},{40,32},{48,40},{56,48},{64,56},{72,6... | collective-permute-start | bytes 148616 | tf_op jit(solution)/shard_map/ppermute | solution.py:17
  17.7 15.4 %collective-permute-start.2 = (f32[129,6,16,1]{0,2,3,1:T(8,128)S(1)}, f32[129,6,16,1]{0,2,3,1:T(8,128)S(1)}, u32[]{:S(2)}, u32[]{:S(2)}) collective-permute-start(f32[129,6,16,1]{0,2,3,1:T(8,128)S(1)} %copy.73), channel_id=1, source_target_pairs={{0,8},{8,16},{16,24},{24,32},{32,40},{40,48},{48,56},{56,64},{64,7... | collective-permute-start | bytes 148616 | tf_op jit(solution)/shard_map/ppermute | solution.py:14
  18.8 14.4 %collective-permute-start = (f32[129,6,1,32]{0,3,2,1:T(8,128)S(1)}, f32[129,6,1,32]{0,3,2,1:T(8,128)S(1)}, u32[]{:S(2)}, u32[]{:S(2)}) collective-permute-start(f32[129,6,1,32]{0,3,2,1:T(8,128)S(1)} %get-tuple-element.18), channel_id=1, source_target_pairs={{0,1},{1,2},{2,3},{3,4},{4,5},{5,6},{6,7},{8,9},{9,10},{10,11},{11... | collective-permute-start | bytes 297224 | tf_op jit(solution)/shard_map/ppermute | solution.py:14
  22.8 10.5 %copy-start = (f32[129,6,16,32]{0,3,2,1:T(8,128)S(1)}, f32[129,6,16,32]{0,3,2,1:T(8,128)}, u32[]{:S(2)}) copy-start(f32[129,6,16,32]{0,3,2,1:T(8,128)} %param.5) | copy-start | bytes 4755460
  22.8 10.4 %collective-permute-start.1 = (f32[129,6,1,32]{0,3,2,1:T(8,128)S(1)}, f32[129,6,1,32]{0,3,2,1:T(8,128)S(1)}, u32[]{:S(2)}, u32[]{:S(2)}) collective-permute-start(f32[129,6,1,32]{0,3,2,1:T(8,128)S(1)} %get-tuple-element.19), channel_id=1, source_target_pairs={{1,0},{2,1},{3,2},{4,3},{5,4},{6,5},{7,6},{9,8},{10,9},{11,10},{12... | collective-permute-start | bytes 297224 | tf_op jit(solution)/shard_map/ppermute | solution.py:17
  35.8 5.2 %copy-start.3 = (f32[129,6,16,32]{0,3,2,1:T(8,128)}, f32[129,6,16,32]{0,3,2,1:T(8,128)S(1)}, u32[]{:S(2)}) copy-start(f32[129,6,16,32]{0,3,2,1:T(8,128)S(1)} %get-tuple-element.16) | copy-start | bytes 4755460
  35.8 10.3 %copy-start.1 = (f32[129,6,16,32]{0,3,2,1:T(8,128)}, f32[129,6,16,32]{0,3,2,1:T(8,128)S(1)}, u32[]{:S(2)}) copy-start(f32[129,6,16,32]{0,3,2,1:T(8,128)S(1)} %get-tuple-element.17) | copy-start | bytes 4755460
  35.8 15.7 %copy-start.5 = (f32[129,6,16,32]{0,3,2,1:T(8,128)}, f32[129,6,16,32]{0,3,2,1:T(8,128)S(1)}, u32[]{:S(2)}) copy-start(f32[129,6,16,32]{0,3,2,1:T(8,128)S(1)} %get-tuple-element.15) | copy-start | bytes 4755460
  35.8 15.7 %copy-start.6 = (f32[129,6,16,32]{0,3,2,1:T(8,128)}, f32[129,6,16,32]{0,3,2,1:T(8,128)S(1)}, u32[]{:S(2)}) copy-start(f32[129,6,16,32]{0,3,2,1:T(8,128)S(1)} %get-tuple-element.14) | copy-start | bytes 4755460
  57.3 2.4 copy-start.4
  57.4 3.3 copy-start.2
  59.7 2.3 copy-start.7
  371.7 2.8 copy-start.8
  373.1 2.8 slice-start
  378.3 3.2 copy-start.9
Sparse Core Ops, SparseCore 0:
  57.5 244.7 all-reduce.2
where the time goes:
time: 394 us; the launch traced here: 389 us
  waiting for transfers between devices  239 us (61%)
  other arithmetic  59.7 us (15%)
  matrix products  40.3 us (10%)
  local copies, waits for them, and re-layouts  17.7 us (4%)
  between operations  16.6 us (4%)
  starting transfers between devices  15.2 us (4%)
    psum x1, waiting for transfers between devices, shards(): gram_total = lax.psum(gram_local, ('lon', 'lat'))  239 us
    dot_general x5, matrix products, shards(): jnp.dot(flat_rows, flat_rows.T, precision=lax.Precision.HIGHEST)  29.4 us
    another operation x4, other arithmetic, shards(): upper_factor = jnp.linalg.cholesky(gram_total).T  22.3 us
    another operation x3, other arithmetic, reduced_operators(): back_factor = jnp.linalg.cholesky(gram_total[1:, 1:])  12.4 us
    ppermute x2, starting transfers between devices, with_halo(): lax.ppermute(lax.slice_in_dim(block, 0, width, axis=dim), axis, backward)  11.1 us
    another operation x2, other arithmetic, reduced_operators(): jax.scipy.linalg.solve_triangular(back_factor, mixed_block.T, lower=True)  10.8 us
    another operation x2, other arithmetic, shards(): jax.scipy.linalg.solve_triangular(head_block.T, flat_rows, lower=True)  9.82 us
    another operation x5, matrix products, shards(): jax.scipy.linalg.solve_triangular(head_block.T, flat_rows, lower=True)  8.3 us
  transfers between devices with their start and end apart: 5, of which 1 were waited for; matrix products, arithmetic and copies ran while one was open for 4% of the time, Pallas kernels for 0%

commit v1 on v0

--- a/solution.py
+++ b/solution.py
@@ -56,7 +56,7 @@
         flat_rows = feature_slab.reshape(states, -1)
         gram_local = gram_local + jnp.dot(flat_rows, flat_rows.T, precision=lax.Precision.HIGHEST)
     gram_local = gram_local / rows_total
-    gram_total = lax.psum(gram_local, ("lon", "lat"))
+    gram_total = jnp.sum(lax.all_gather(gram_local, ("lon", "lat")), axis=0)
     upper_factor = jnp.linalg.cholesky(gram_total).T
     forward_operator, backward_operator = reduced_operators(upper_factor, gram_total)
     head_block = upper_factor[:snap_count, :snap_count]

time: 394 us -> 334 us (0.85)
  waiting for transfers between devices: 239 us -> 149 us
  other arithmetic: 59.7 us -> 74.7 us
  matrix products: 40.3 us -> 53.3 us
    psum x1 -> x0, waiting for transfers between devices: 239 us -> none  [shards(): gram_total = lax.psum(gram_local, ('lon', 'lat'))]
    all_gather x0 -> x1, waiting for transfers between devices: none -> 149 us  [shards(): gram_total = jnp.sum(lax.all_gather(gram_local, ('lon', 'lat')), axis=0)]
    dot_general x5, matrix products: 29.4 us -> 42.7 us  [shards(): jnp.dot(flat_rows, flat_rows.T, precision=lax.Precision.HIGHEST)]
    reduce_sum x0 -> x1, other arithmetic: none -> 12.5 us  [shards(): gram_total = jnp.sum(lax.all_gather(gram_local, ('lon', 'lat')), axis=0)]
where the time goes in v1:
time: 334 us; the launch traced here: 328 us
  waiting for transfers between devices  149 us (45%)
  other arithmetic  74.7 us (22%)
  matrix products  53.3 us (16%)
  local copies, waits for them, and re-layouts  19.3 us (6%)
  between operations  16.9 us (5%)
  starting transfers between devices  15.2 us (5%)
    all_gather x1, waiting for transfers between devices, shards(): gram_total = jnp.sum(lax.all_gather(gram_local, ('lon', 'lat')), axis=0)  149 us
    dot_general x5, matrix products, shards(): jnp.dot(flat_rows, flat_rows.T, precision=lax.Precision.HIGHEST)  42.7 us
    another operation x4, other arithmetic, shards(): upper_factor = jnp.linalg.cholesky(gram_total).T  26 us
    reduce_sum x1, other arithmetic, shards(): gram_total = jnp.sum(lax.all_gather(gram_local, ('lon', 'lat')), axis=0)  12.5 us
    another operation x3, other arithmetic, reduced_operators(): back_factor = jnp.linalg.cholesky(gram_total[1:, 1:])  12.4 us
    ppermute x2, starting transfers between devices, with_halo(): lax.ppermute(lax.slice_in_dim(block, 0, width, axis=dim), axis, backward)  11.1 us
    another operation x2, other arithmetic, reduced_operators(): jax.scipy.linalg.solve_triangular(back_factor, mixed_block.T, lower=True)  10.5 us
    another operation x2, other arithmetic, shards(): jax.scipy.linalg.solve_triangular(head_block.T, flat_rows, lower=True)  9.82 us
  transfers between devices with their start and end apart: 5, of which 1 were waited for; matrix products, arithmetic and copies ran while one was open for 4% of the time, Pallas kernels for 0%

profile of v1, /device:TPU:1, one launch (start us, length us, event | category | flops | bytes accessed | tf_op | source)
XLA Modules:
  0.0 327.9 jit_solution(17309855305233095214)
XLA Ops:
  7.2 1.5 fusion.35
  8.8 8.9 %collective-permute-start.3 = (f32[129,6,16,1]{0,2,3,1:T(8,128)S(1)}, f32[129,6,16,1]{0,2,3,1:T(8,128)S(1)}, u32[]{:S(2)}, u32[]{:S(2)}) collective-permute-start(f32[129,6,16,1]{0,2,3,1:T(8,128)S(1)} %copy.53), channel_id=1, source_target_pairs={{8,0},{16,8},{24,16},{32,24},{40,32},{48,40},{56,48},{64,56},{72,6... | collective-permute-start | bytes 148616 | tf_op jit(solution)/shard_map/ppermute | solution.py:17
  17.8 1.1 fusion.34
  18.8 4.0 %collective-permute-start = (f32[129,6,1,32]{0,3,2,1:T(8,128)S(1)}, f32[129,6,1,32]{0,3,2,1:T(8,128)S(1)}, u32[]{:S(2)}, u32[]{:S(2)}) collective-permute-start(f32[129,6,1,32]{0,3,2,1:T(8,128)S(1)} %get-tuple-element.18), channel_id=1, source_target_pairs={{0,1},{1,2},{2,3},{3,4},{4,5},{5,6},{6,7},{8,9},{9,10},{10,11},{11... | collective-permute-start | bytes 297224 | tf_op jit(solution)/shard_map/ppermute | solution.py:14
  22.8 2.2 collective-permute-start.1
  25.0 8.0 %convolution_bitcast_fusion.4 = f32[129,129]{1,0:T(8,128)S(1)} fusion(f32[129,6,16,32]{0,3,2,1:T(8,128)} %param.5), kind=kOutput, calls=%fused_computation.12 | convolution fusion | flops 613453824 | bytes 1651716 | tf_op jit(solution)/shard_map/dot_general | solution.py:57
  33.3 2.6 fusion.3
  35.9 5.3 %convolution_bitcast_fusion.2 = f32[129,129]{1,0:T(8,128)S(1)} fusion(f32[129,6,16,32]{0,3,2,1:T(8,128)S(1)} %get-tuple-element.15), kind=kOutput, calls=%fused_computation.10 | convolution fusion | flops 613453824 | bytes 1651716 | tf_op jit(solution)/shard_map/dot_general | solution.py:57
  41.2 5.3 %convolution_bitcast_fusion.1 = f32[129,129]{1,0:T(8,128)S(1)} fusion(f32[129,6,16,32]{0,3,2,1:T(8,128)S(1)} %get-tuple-element.16), kind=kOutput, calls=%fused_computation.9 | convolution fusion | flops 613453824 | bytes 1651716 | tf_op jit(solution)/shard_map/dot_general | solution.py:57
  46.4 18.3 %convolution_bitcast_fusion = f32[129,129]{1,0:T(8,128)S(1)} fusion(f32[129,6,16,32]{0,3,2,1:T(8,128)S(1)} %get-tuple-element.17), kind=kOutput, calls=%fused_computation.8 | convolution fusion | flops 613453824 | bytes 1651716 | tf_op jit(solution)/shard_map/dot_general | solution.py:57
  64.7 5.9 %fusion.9 = f32[1,129,129]{2,1,0:T(8,128)} fusion(f32[129,129]{1,0:T(8,128)S(1)} %convolution_bitcast_fusion, f32[129,129]{1,0:T(8,128)S(1)} %convolution_bitcast_fusion.1, f32[129,129]{1,0:T(8,128)S(1)} %convolution_bitcast_fusion.2, f32[129,129]{1,0:T(8,128)S(1)} %convolution_bitcast_fusion.4, f32[129,6,16,32]{0,3,2,1:T(8,128)S(1)} %get-tuple-element.14), kind=kOutput, calls=%fused_computation.18 | convolution fusion | flops 613537024 | bytes 1917972 | tf_op jit(solution)/shard_map/dot_general | solution.py:57
  70.7 1.7 slice.141
  74.0 1.3 slice.143
  75.3 1.3 slice.140
  76.6 148.6 %all-gather.4.cloned.1.call-done = f32[256,129,129]{2,1,0:T(8,128)} async-done(((f32[1,129,129]{2,1,0:T(8,128)}), f32[256,129,129]{2,1,0:T(8,128)}) %all-gather.4.cloned.1.call-update) | async-done | bytes 17040400 | tf_op jit(solution)/shard_map/all_gather | solution.py:59
  225.2 12.5 %reduce_sum.9 = f32[129,129]{1,0:T(8,128)S(1)} reduce(f32[256,129,129]{2,1,0:T(8,128)} %all-gather.4.cloned.1.call-done, f32[]{:T(128)} %constant.99.clone.1), dimensions={0}, to_apply=%region_0.0 | reduce | flops 4243455 | bytes 17106952 | tf_op jit(solution)/shard_map/reduce_sum | solution.py:59
  239.2 12.5 %cholesky.63 = f32[128,128]{1,0:T(8,128)S(1)} custom-call(f32[128,128]{1,0:T(8,128)} %cholesky.152), custom_call_target="Cholesky" | custom-call | tf_op jit(solution)/shard_map/jit(cholesky)/cholesky | solution.py:60
  251.7 1.2 select_reduce_fusion.1
  253.8 11.7 %cholesky.144 = f32[128,128]{1,0:T(8,128)S(1)} custom-call(f32[128,128]{1,0:T(8,128)S(1)} %fusion.17), custom_call_target="Cholesky" | custom-call | tf_op jit(solution)/shard_map/jit(cholesky)/cholesky | solution.py:28
  266.9 9.8 %custom-call.31 = f32[1,128,128]{1,2,0:T(8,128)S(1)} custom-call(f32[1,128,128]{2,1,0:T(8,128)S(1)} %fusion.11), custom_call_target="InvertDiagBlocksLowerTriangular" | custom-call | tf_op jit(solution)/shard_map/jit(_solve_triangular)/triangular_solve | solution.py:32
  278.0 1.4 compare_reduce_fusion.1
  279.4 10.8 %custom-call.17 = f32[1,128,128]{1,2,0:T(8,128)S(1)} custom-call(f32[1,128,128]{2,1,0:T(8,128)} %get-tuple-element.23), custom_call_target="InvertDiagBlocksLowerTriangular" | custom-call | tf_op jit(solution)/shard_map/jit(cholesky)/cholesky | solution.py:60
  290.2 1.4 fusion.33
  292.9 1.3 cholesky.140
  294.2 1.3 cholesky.141
  297.2 9.8 %custom-call.24 = f32[1,128,128]{1,2,0:T(8,128)S(1)} custom-call(f32[1,128,128]{2,1,0:T(8,128)S(1)} %fusion.14), custom_call_target="InvertDiagBlocksLowerTriangular" | custom-call | tf_op jit(solution)/shard_map/jit(_solve_triangular)/triangular_solve | solution.py:66
  308.0 2.8 fusion.25
  310.8 1.4 fusion.23
  312.2 1.4 fusion.21
  313.6 1.4 fusion.19
  315.0 1.4 fusion.27
  317.4 3.2 copy-done.9
  (58 shorter events, 9.9 us)
Async XLA Ops:
  7.2 218.0 %all-gather.4.cloned.1.call-start = ((), (), s32[]{:S(2)}) async-start(), calls=%async_computation | async-start | bytes 35790848 | tf_op jit(solution)/shard_map/all_gather | solution.py:59
  8.8 24.2 %collective-permute-start.3 = (f32[129,6,16,1]{0,2,3,1:T(8,128)S(1)}, f32[129,6,16,1]{0,2,3,1:T(8,128)S(1)}, u32[]{:S(2)}, u32[]{:S(2)}) collective-permute-start(f32[129,6,16,1]{0,2,3,1:T(8,128)S(1)} %copy.53), channel_id=1, source_target_pairs={{8,0},{16,8},{24,16},{32,24},{40,32},{48,40},{56,48},{64,56},{72,6... | collective-permute-start | bytes 148616 | tf_op jit(solution)/shard_map/ppermute | solution.py:17
  17.7 15.4 %collective-permute-start.2 = (f32[129,6,16,1]{0,2,3,1:T(8,128)S(1)}, f32[129,6,16,1]{0,2,3,1:T(8,128)S(1)}, u32[]{:S(2)}, u32[]{:S(2)}) collective-permute-start(f32[129,6,16,1]{0,2,3,1:T(8,128)S(1)} %copy.52), channel_id=1, source_target_pairs={{0,8},{8,16},{16,24},{24,32},{32,40},{40,48},{48,56},{56,64},{64,7... | collective-permute-start | bytes 148616 | tf_op jit(solution)/shard_map/ppermute | solution.py:14
  18.8 14.4 %collective-permute-start = (f32[129,6,1,32]{0,3,2,1:T(8,128)S(1)}, f32[129,6,1,32]{0,3,2,1:T(8,128)S(1)}, u32[]{:S(2)}, u32[]{:S(2)}) collective-permute-start(f32[129,6,1,32]{0,3,2,1:T(8,128)S(1)} %get-tuple-element.18), channel_id=1, source_target_pairs={{0,1},{1,2},{2,3},{3,4},{4,5},{5,6},{6,7},{8,9},{9,10},{10,11},{11... | collective-permute-start | bytes 297224 | tf_op jit(solution)/shard_map/ppermute | solution.py:14
  22.8 10.5 %copy-start = (f32[129,6,16,32]{0,3,2,1:T(8,128)S(1)}, f32[129,6,16,32]{0,3,2,1:T(8,128)}, u32[]{:S(2)}) copy-start(f32[129,6,16,32]{0,3,2,1:T(8,128)} %param.5) | copy-start | bytes 4755460
  22.8 10.4 %collective-permute-start.1 = (f32[129,6,1,32]{0,3,2,1:T(8,128)S(1)}, f32[129,6,1,32]{0,3,2,1:T(8,128)S(1)}, u32[]{:S(2)}, u32[]{:S(2)}) collective-permute-start(f32[129,6,1,32]{0,3,2,1:T(8,128)S(1)} %get-tuple-element.19), channel_id=1, source_target_pairs={{1,0},{2,1},{3,2},{4,3},{5,4},{6,5},{7,6},{9,8},{10,9},{11,10},{12... | collective-permute-start | bytes 297224 | tf_op jit(solution)/shard_map/ppermute | solution.py:17
  35.8 5.3 %copy-start.3 = (f32[129,6,16,32]{0,3,2,1:T(8,128)}, f32[129,6,16,32]{0,3,2,1:T(8,128)S(1)}, u32[]{:S(2)}) copy-start(f32[129,6,16,32]{0,3,2,1:T(8,128)S(1)} %get-tuple-element.16) | copy-start | bytes 4755460
  35.8 10.6 %copy-start.1 = (f32[129,6,16,32]{0,3,2,1:T(8,128)}, f32[129,6,16,32]{0,3,2,1:T(8,128)S(1)}, u32[]{:S(2)}) copy-start(f32[129,6,16,32]{0,3,2,1:T(8,128)S(1)} %get-tuple-element.17) | copy-start | bytes 4755460
  35.9 28.8 %copy-start.5 = (f32[129,6,16,32]{0,3,2,1:T(8,128)}, f32[129,6,16,32]{0,3,2,1:T(8,128)S(1)}, u32[]{:S(2)}) copy-start(f32[129,6,16,32]{0,3,2,1:T(8,128)S(1)} %get-tuple-element.15) | copy-start | bytes 4755460
  35.9 28.8 %copy-start.6 = (f32[129,6,16,32]{0,3,2,1:T(8,128)}, f32[129,6,16,32]{0,3,2,1:T(8,128)S(1)}, u32[]{:S(2)}) copy-start(f32[129,6,16,32]{0,3,2,1:T(8,128)S(1)} %get-tuple-element.14) | copy-start | bytes 4755460
  70.7 2.4 copy-start.4
  70.7 3.3 %copy-start.2 = (f32[129,6,16,32]{0,3,2,1:T(8,128)S(1)}, f32[129,6,16,32]{0,3,2,1:T(8,128)}, u32[]{:S(2)}) copy-start(f32[129,6,16,32]{0,3,2,1:T(8,128)} %copy-done.1) | copy-start | bytes 4755460
  73.0 2.3 copy-start.7
  237.9 0.7 copy-start.10
  310.8 2.8 copy-start.8
  312.2 2.8 slice-start
  317.4 3.2 copy-start.9
Sparse Core Ops, SparseCore 0:
  70.8 154.3 all-gather.3
